TPU v7x, 32 devices: a whole 2x2x4 slice. The times are simulated.
32 devices in a mesh: pipe: 4 (over y, x), ctx: 8 (over z, core).
Axes of the slice: x: 2, y: 2, z: 4, core: 2. Of those that a mesh axis runs over, the one named last changes fastest.
Arguments:
- activations: bfloat16 [4, 1024, 4096], P('pipe', 'ctx'), may hold values from -17 to 17
- gate_values: bfloat16 [4, 1024, 4096], P('pipe', 'ctx'), may hold values from -6 to 6
- out_grad: bfloat16 [4, 1024, 4096], P('pipe', 'ctx'), may hold values from -6 to 6
- filters: float32 [4, 256, 128], P('pipe'), may hold values from -0.26516503 to 0.26516503
- norm_gain: float32 [4, 4096], P('pipe'), may hold values from 0.1 to 1.9
- doc_ids: int32 [4, 1024], P('pipe'), may hold values from 0 to 7, never falling along the last dimension, each value on 1 to 256 neighbouring positions
Outputs:
- prev_grad: bfloat16 [4, 1024, 4096], P('pipe', 'ctx')
- gain_grad: float32 [4, 4096], P('pipe')
Inputs may be any that keep to these rules, and one draw needn't show every extreme that they name: `doc_ids`: along each section's tokens the document number never falls; a document covers 1 to 256 tokens, and every number from 0 up is used.
All inputs are finite; a program needn't handle non-finite values.
Results may differ from a plain program's by a relative error of at most 0.0042.
Values may be sent and summed in bfloat16 or wider, within the bound.
A program may use at most 64 MiB of HBM per device.

v0:
```python
import math

import jax
import jax.numpy as jnp
from jax import lax
from jax.sharding import PartitionSpec as P


def from_behind(value, axis, steps):
    count = lax.axis_size(axis)
    initial, last = (max(0, -steps), min(count, count - steps))
    return lax.ppermute(value, axis, [(source, source + steps) for source in range(initial, last)])


def shifted(value, axis, by):
    peers = lax.axis_size(axis)
    return lax.ppermute(value, axis, [(i, (i + by) % peers) for i in range(peers)])


def toeplitz_mix(rows, row_ids, out_ids, filter_rows, count_rows):
    span = rows.shape[0]
    channels = rows.shape[1]
    groups = filter_rows.shape[0]
    taps = filter_rows.shape[1]
    group_size = channels // groups
    block = math.gcd(groups, 32)
    blocks = groups // block
    same_doc = out_ids[:, None] == row_ids[None, :]
    padded = jnp.concatenate(
        [filter_rows, jnp.zeros((groups, span + 1 - taps), jnp.float32)], axis=1
    )
    filter_blocks = padded.reshape(blocks, block, span + 1)
    by_channel = rows.T.reshape(blocks, block, group_size, span)

    def one_block(operands):
        filter_part, row_part = operands
        tiled = jnp.tile(filter_part, (1, count_rows))[:, : count_rows * span]
        banded = tiled.reshape(block, count_rows, span)
        banded = jnp.where(same_doc[None], banded, 0.0)
        return jnp.einsum(
            "gcj,gtj->gct", row_part.astype(jnp.float32), banded, precision=lax.Precision.HIGHEST
        )

    mixed = lax.map(one_block, (filter_blocks, by_channel))
    return mixed.reshape(channels, count_rows).T


def on_device(activations, gate_values, out_grad, filters, norm_gain, doc_ids):
    tokens_dev = activations.shape[1]
    reach = filters.shape[2] - 1
    filter_rows = filters[0]
    all_ids = doc_ids[0]
    first_row = lax.axis_index("ctx") * tokens_dev
    own_ids = lax.dynamic_slice_in_dim(all_ids, first_row, tokens_dev)
    features = activations[0].astype(jnp.float32)
    inv_rms = lax.rsqrt(jnp.mean(features * features, axis=-1, keepdims=True) + 1e-06)
    normed = features * inv_rms
    upstream = out_grad[0].astype(jnp.float32)
    hidden_grad = (upstream * gate_values[0].astype(jnp.float32)).astype(jnp.bfloat16)
    padded_ids = jnp.concatenate([all_ids, jnp.full((reach,), -1, jnp.int32)])
    next_ids = lax.dynamic_slice_in_dim(padded_ids, first_row + tokens_dev, reach)
    tail_rows = from_behind(hidden_grad[:reach], "ctx", -1)
    extended = jnp.concatenate([hidden_grad, tail_rows], axis=0)
    mixed_grad = toeplitz_mix(
        extended, jnp.concatenate([own_ids, next_ids]), own_ids, filter_rows, tokens_dev
    )
    gain_grad = lax.psum(jnp.sum(mixed_grad * normed, axis=0), "ctx")
    scaled = mixed_grad * norm_gain[0]
    projection = jnp.mean(scaled * normed, axis=-1, keepdims=True)
    input_grad = (upstream + inv_rms * (scaled - normed * projection)).astype(jnp.bfloat16)
    prev_grad = shifted(input_grad, "pipe", -1)
    return (prev_grad[None], gain_grad[None])


def solution(mesh):
    return jax.shard_map(
        on_device,
        mesh=mesh,
        in_specs=(
            P("pipe", "ctx", None),
            P("pipe", "ctx", None),
            P("pipe", "ctx", None),
            P("pipe", None, None),
            P("pipe", None),
            P("pipe", None),
        ),
        out_specs=(P("pipe", "ctx", None), P("pipe", None)),
        check_vma=False,
    )
```

profile of v0, /device:TPU:0, one launch (start us, length us, event | category | flops | bytes accessed | tf_op | source)
XLA Modules:
  0.0 215.5 jit_solution(15813863769774888173)
XLA Ops:
  8.0 3.0 %pad_maximum_fusion = bf16[255,4096]{0,1:T(8,128)(2,1)} fusion(bf16[127,4096]{0,1:T(8,128)(2,1)} %collective-permute-done, bf16[128,4096]{0,1:T(8,128)(2,1)S(1)} %fusion.19), kind=kLoop, calls=%fused_computation.27 | loop fusion | flops 4177920 | bytes 4177920 | tf_op jit(solution)/shard_map/concatenate | solution.py:63
  11.1 157.9 %while.11 = (s32[]{:T(128)}, f32[8,32,16,128]{3,2,1,0:T(8,128)}, bf16[8,32,16,255]{3,2,1,0:T(8,128)(2,1)}, f32[8,32,256]{2,1,0:T(8,128)S(1)}, s32[255]{0:T(256)S(1)}, /*index=5*/s32[128]{0:T(128)S(1)}, s32[]{:T(128)}) while((s32[]{:T(128)}, f32[8,32,16,128]{3,2,1,0:T(8,128)}, bf16[8,32,16,255]{3,2,1,0:T(8,128)(2,1)}, ...), condition=%wide.region_2.3_spmd.clone, body=%wide.region_1.2_spmd.clone.sunk | while | flops 201617280 | bytes 34179404 | solution.py:44
  11.4 2.4 %copy.16 = f32[4,8,128,256]{3,1,2,0:T(8,128)S(1)} copy(f32[4,8,128,256]{3,2,1,0:T(8,128)S(1)} %bitcast.55) | data formatting | bytes 8388608 | tf_op jit(solution)/shard_map/while
  13.8 2.2 %slice.11 = f32[32,32640]{1,0:T(8,128)} slice(f32[32,32768]{1,0:T(8,128)S(1)} %bitcast.56), slice={[0:32], [0:32640]} | slice | bytes 8355840 | tf_op jit(solution)/shard_map/while/body/eval_jaxpr/slice | solution.py:37
  16.1 9.4 %reshape.52 = f32[32,128,255]{2,1,0:T(8,128)} reshape(f32[32,32640]{1,0:T(8,128)} %slice.11) | data formatting | bytes 8355840 | tf_op jit(solution)/shard_map/while/body/eval_jaxpr/reshape | solution.py:38
  25.5 5.2 %fusion.31 = f32[8,32,16,128]{3,2,1,0:T(8,128)} fusion(f32[8,32,16,128]{3,2,1,0:T(8,128)} %get-tuple-element.113, s32[]{:T(128)} %get-tuple-element.112, f32[32,128,255]{2,1,0:T(8,128)} %reshape.52, pred[128,255]{1,0:T(8,128)(4,1)S(1)} %broadcast_compare_fusion.2, bf16[8,32,16,255]{3,2,1,0:T(8,128)(2,1)} %get-tuple-element.121), kind=kOutput, calls=%fused_computation.6.clone.1 | convolution fusion | flops 201584640 | bytes 4752256 | tf_op jit(solution)/shard_map/while/body/eval_jaxpr/gcj,gtj->gct/dot_general | solution.py:40
  31.1 2.4 %copy.16 = f32[4,8,128,256]{3,1,2,0:T(8,128)S(1)} copy(f32[4,8,128,256]{3,2,1,0:T(8,128)S(1)} %bitcast.55) | data formatting | bytes 8388608 | tf_op jit(solution)/shard_map/while
  33.6 2.2 %slice.11 = f32[32,32640]{1,0:T(8,128)} slice(f32[32,32768]{1,0:T(8,128)S(1)} %bitcast.56), slice={[0:32], [0:32640]} | slice | bytes 8355840 | tf_op jit(solution)/shard_map/while/body/eval_jaxpr/slice | solution.py:37
  35.8 9.4 %reshape.52 = f32[32,128,255]{2,1,0:T(8,128)} reshape(f32[32,32640]{1,0:T(8,128)} %slice.11) | data formatting | bytes 8355840 | tf_op jit(solution)/shard_map/while/body/eval_jaxpr/reshape | solution.py:38
  45.3 5.3 %fusion.31 = f32[8,32,16,128]{3,2,1,0:T(8,128)} fusion(f32[8,32,16,128]{3,2,1,0:T(8,128)} %get-tuple-element.113, s32[]{:T(128)} %get-tuple-element.112, f32[32,128,255]{2,1,0:T(8,128)} %reshape.52, pred[128,255]{1,0:T(8,128)(4,1)S(1)} %broadcast_compare_fusion.2, bf16[8,32,16,255]{3,2,1,0:T(8,128)(2,1)} %get-tuple-element.121), kind=kOutput, calls=%fused_computation.6.clone.1 | convolution fusion | flops 201584640 | bytes 4752256 | tf_op jit(solution)/shard_map/while/body/eval_jaxpr/gcj,gtj->gct/dot_general | solution.py:40
  50.9 2.4 %copy.16 = f32[4,8,128,256]{3,1,2,0:T(8,128)S(1)} copy(f32[4,8,128,256]{3,2,1,0:T(8,128)S(1)} %bitcast.55) | data formatting | bytes 8388608 | tf_op jit(solution)/shard_map/while
  53.3 2.2 %slice.11 = f32[32,32640]{1,0:T(8,128)} slice(f32[32,32768]{1,0:T(8,128)S(1)} %bitcast.56), slice={[0:32], [0:32640]} | slice | bytes 8355840 | tf_op jit(solution)/shard_map/while/body/eval_jaxpr/slice | solution.py:37
  55.6 9.4 %reshape.52 = f32[32,128,255]{2,1,0:T(8,128)} reshape(f32[32,32640]{1,0:T(8,128)} %slice.11) | data formatting | bytes 8355840 | tf_op jit(solution)/shard_map/while/body/eval_jaxpr/reshape | solution.py:38
  65.0 5.3 %fusion.31 = f32[8,32,16,128]{3,2,1,0:T(8,128)} fusion(f32[8,32,16,128]{3,2,1,0:T(8,128)} %get-tuple-element.113, s32[]{:T(128)} %get-tuple-element.112, f32[32,128,255]{2,1,0:T(8,128)} %reshape.52, pred[128,255]{1,0:T(8,128)(4,1)S(1)} %broadcast_compare_fusion.2, bf16[8,32,16,255]{3,2,1,0:T(8,128)(2,1)} %get-tuple-element.121), kind=kOutput, calls=%fused_computation.6.clone.1 | convolution fusion | flops 201584640 | bytes 4752256 | tf_op jit(solution)/shard_map/while/body/eval_jaxpr/gcj,gtj->gct/dot_general | solution.py:40
  70.6 2.4 %copy.16 = f32[4,8,128,256]{3,1,2,0:T(8,128)S(1)} copy(f32[4,8,128,256]{3,2,1,0:T(8,128)S(1)} %bitcast.55) | data formatting | bytes 8388608 | tf_op jit(solution)/shard_map/while
  75.3 9.4 %reshape.52 = f32[32,128,255]{2,1,0:T(8,128)} reshape(f32[32,32640]{1,0:T(8,128)} %slice.11) | data formatting | bytes 8355840 | tf_op jit(solution)/shard_map/while/body/eval_jaxpr/reshape | solution.py:38
  84.8 5.2 %fusion.31 = f32[8,32,16,128]{3,2,1,0:T(8,128)} fusion(f32[8,32,16,128]{3,2,1,0:T(8,128)} %get-tuple-element.113, s32[]{:T(128)} %get-tuple-element.112, f32[32,128,255]{2,1,0:T(8,128)} %reshape.52, pred[128,255]{1,0:T(8,128)(4,1)S(1)} %broadcast_compare_fusion.2, bf16[8,32,16,255]{3,2,1,0:T(8,128)(2,1)} %get-tuple-element.121), kind=kOutput, calls=%fused_computation.6.clone.1 | convolution fusion | flops 201584640 | bytes 4752256 | tf_op jit(solution)/shard_map/while/body/eval_jaxpr/gcj,gtj->gct/dot_general | solution.py:40
  90.4 2.4 %copy.16 = f32[4,8,128,256]{3,1,2,0:T(8,128)S(1)} copy(f32[4,8,128,256]{3,2,1,0:T(8,128)S(1)} %bitcast.55) | data formatting | bytes 8388608 | tf_op jit(solution)/shard_map/while
  95.0 9.4 %reshape.52 = f32[32,128,255]{2,1,0:T(8,128)} reshape(f32[32,32640]{1,0:T(8,128)} %slice.11) | data formatting | bytes 8355840 | tf_op jit(solution)/shard_map/while/body/eval_jaxpr/reshape | solution.py:38
  104.5 5.2 %fusion.31 = f32[8,32,16,128]{3,2,1,0:T(8,128)} fusion(f32[8,32,16,128]{3,2,1,0:T(8,128)} %get-tuple-element.113, s32[]{:T(128)} %get-tuple-element.112, f32[32,128,255]{2,1,0:T(8,128)} %reshape.52, pred[128,255]{1,0:T(8,128)(4,1)S(1)} %broadcast_compare_fusion.2, bf16[8,32,16,255]{3,2,1,0:T(8,128)(2,1)} %get-tuple-element.121), kind=kOutput, calls=%fused_computation.6.clone.1 | convolution fusion | flops 201584640 | bytes 4752256 | tf_op jit(solution)/shard_map/while/body/eval_jaxpr/gcj,gtj->gct/dot_general | solution.py:40
  110.1 2.4 %copy.16 = f32[4,8,128,256]{3,1,2,0:T(8,128)S(1)} copy(f32[4,8,128,256]{3,2,1,0:T(8,128)S(1)} %bitcast.55) | data formatting | bytes 8388608 | tf_op jit(solution)/shard_map/while
  114.8 9.4 %reshape.52 = f32[32,128,255]{2,1,0:T(8,128)} reshape(f32[32,32640]{1,0:T(8,128)} %slice.11) | data formatting | bytes 8355840 | tf_op jit(solution)/shard_map/while/body/eval_jaxpr/reshape | solution.py:38
  124.2 5.2 %fusion.31 = f32[8,32,16,128]{3,2,1,0:T(8,128)} fusion(f32[8,32,16,128]{3,2,1,0:T(8,128)} %get-tuple-element.113, s32[]{:T(128)} %get-tuple-element.112, f32[32,128,255]{2,1,0:T(8,128)} %reshape.52, pred[128,255]{1,0:T(8,128)(4,1)S(1)} %broadcast_compare_fusion.2, bf16[8,32,16,255]{3,2,1,0:T(8,128)(2,1)} %get-tuple-element.121), kind=kOutput, calls=%fused_computation.6.clone.1 | convolution fusion | flops 201584640 | bytes 4752256 | tf_op jit(solution)/shard_map/while/body/eval_jaxpr/gcj,gtj->gct/dot_general | solution.py:40
  129.8 2.4 %copy.16 = f32[4,8,128,256]{3,1,2,0:T(8,128)S(1)} copy(f32[4,8,128,256]{3,2,1,0:T(8,128)S(1)} %bitcast.55) | data formatting | bytes 8388608 | tf_op jit(solution)/shard_map/while
  134.5 9.4 %reshape.52 = f32[32,128,255]{2,1,0:T(8,128)} reshape(f32[32,32640]{1,0:T(8,128)} %slice.11) | data formatting | bytes 8355840 | tf_op jit(solution)/shard_map/while/body/eval_jaxpr/reshape | solution.py:38
  143.9 5.2 %fusion.31 = f32[8,32,16,128]{3,2,1,0:T(8,128)} fusion(f32[8,32,16,128]{3,2,1,0:T(8,128)} %get-tuple-element.113, s32[]{:T(128)} %get-tuple-element.112, f32[32,128,255]{2,1,0:T(8,128)} %reshape.52, pred[128,255]{1,0:T(8,128)(4,1)S(1)} %broadcast_compare_fusion.2, bf16[8,32,16,255]{3,2,1,0:T(8,128)(2,1)} %get-tuple-element.121), kind=kOutput, calls=%fused_computation.6.clone.1 | convolution fusion | flops 201584640 | bytes 4752256 | tf_op jit(solution)/shard_map/while/body/eval_jaxpr/gcj,gtj->gct/dot_general | solution.py:40
  149.5 2.4 %copy.16 = f32[4,8,128,256]{3,1,2,0:T(8,128)S(1)} copy(f32[4,8,128,256]{3,2,1,0:T(8,128)S(1)} %bitcast.55) | data formatting | bytes 8388608 | tf_op jit(solution)/shard_map/while
  154.2 9.4 %reshape.52 = f32[32,128,255]{2,1,0:T(8,128)} reshape(f32[32,32640]{1,0:T(8,128)} %slice.11) | data formatting | bytes 8355840 | tf_op jit(solution)/shard_map/while/body/eval_jaxpr/reshape | solution.py:38
  163.7 5.3 %fusion.31 = f32[8,32,16,128]{3,2,1,0:T(8,128)} fusion(f32[8,32,16,128]{3,2,1,0:T(8,128)} %get-tuple-element.113, s32[]{:T(128)} %get-tuple-element.112, f32[32,128,255]{2,1,0:T(8,128)} %reshape.52, pred[128,255]{1,0:T(8,128)(4,1)S(1)} %broadcast_compare_fusion.2, bf16[8,32,16,255]{3,2,1,0:T(8,128)(2,1)} %get-tuple-element.121), kind=kOutput, calls=%fused_computation.6.clone.1 | convolution fusion | flops 201584640 | bytes 4752256 | tf_op jit(solution)/shard_map/while/body/eval_jaxpr/gcj,gtj->gct/dot_general | solution.py:40
  168.9 2.6 %fusion.24 = (f32[4096]{0:T(1024)S(1)}, f32[128]{0:T(128)S(1)}) fusion(f32[8,32,16,128]{3,2,1,0:T(8,128)} %get-tuple-element.29, bf16[1,128,4096]{1,2,0:T(8,128)(2,1)S(1)} %copy.11, f32[128]{0:T(128)S(1)} %add_rsqrt_fusion, f32[4096]{0:T(1024)S(1)} %bitcast.62), kind=kLoop, calls=%fused_computation.25 | loop fusion | flops 3665792 | bytes 3179520 | tf_op jit(solution)/shard_map/reduce_sum | solution.py:67
  172.7 4.0 %collective-permute-start.1 = (bf16[128,4096]{0,1:T(8,128)(2,1)S(1)}, bf16[128,4096]{0,1:T(8,128)(2,1)S(1)}, u32[]{:S(2)}, u32[]{:S(2)}) collective-permute-start(bf16[128,4096]{0,1:T(8,128)(2,1)S(1)} %fusion.20), channel_id=1, source_target_pairs={{0,24},{8,0},{16,8},{24,16},{1,25},{9,1},{17,9},{25,17},{2,26},{10... | collective-permute-start | bytes 3145736 | tf_op jit(solution)/shard_map/ppermute | solution.py:17
  176.6 37.6 %psum.7 = f32[1,4096]{1,0:T(1,128)} all-reduce(f32[1,4096]{1,0:T(1,128)S(1)} %bitcast.64), channel_id=1, replica_groups=mesh['pipe'=4,'ctx'=8] {'ctx'}, use_global_device_ids=true, to_apply=%region_5.6 | all-reduce | flops 4096 | bytes 32768 | tf_op jit(solution)/shard_map/psum | solution.py:67
  (56 shorter events, 24.1 us)
Async XLA Ops:
  0.6 1.7 copy-start.1
  3.0 3.3 %copy-start.2 = (f32[1,256,128]{2,1,0:T(8,128)S(1)}, f32[1,256,128]{2,1,0:T(8,128)}, u32[]{:S(2)}) copy-start(f32[1,256,128]{2,1,0:T(8,128)} %param.11) | copy-start | bytes 393220
  3.0 3.3 %copy-start.4 = (s32[1,1024]{1,0:T(1,128)S(1)}, s32[1,1024]{1,0:T(1,128)}, u32[]{:S(2)}) copy-start(s32[1,1024]{1,0:T(1,128)} %param.13) | copy-start | bytes 12292
  3.3 4.7 %collective-permute-start = (bf16[127,4096]{0,1:T(8,128)(2,1)S(1)}, bf16[127,4096]{0,1:T(8,128)(2,1)}, u32[]{:S(2)}, u32[]{:S(2)}) collective-permute-start(bf16[127,4096]{0,1:T(8,128)(2,1)S(1)} %bitcast.58), channel_id=1, source_target_pairs={{1,0},{2,1},{3,2},{4,3},{5,4},{6,5},{7,6},{9,8},{10,9},{11,10},{12... | collective-permute-start | bytes 3121160 | tf_op jit(solution)/shard_map/ppermute | solution.py:12
  11.1 157.9 %copy-start.3 = (f32[1,4096]{1,0:T(1,128)S(1)}, f32[1,4096]{1,0:T(1,128)}, u32[]{:S(2)}) copy-start(f32[1,4096]{1,0:T(1,128)} %param.12) | copy-start | bytes 49156
  168.9 2.7 %copy-start = (f32[8,32,16,128]{3,2,1,0:T(8,128)S(1)}, f32[8,32,16,128]{3,2,1,0:T(8,128)}, u32[]{:S(2)}) copy-start(f32[8,32,16,128]{3,2,1,0:T(8,128)} %get-tuple-element.29) | copy-start | bytes 6291460
  172.7 41.5 %collective-permute-start.1 = (bf16[128,4096]{0,1:T(8,128)(2,1)S(1)}, bf16[128,4096]{0,1:T(8,128)(2,1)S(1)}, u32[]{:S(2)}, u32[]{:S(2)}) collective-permute-start(bf16[128,4096]{0,1:T(8,128)(2,1)S(1)} %fusion.20), channel_id=1, source_target_pairs={{0,24},{8,0},{16,8},{24,16},{1,25},{9,1},{17,9},{25,17},{2,26},{10... | collective-permute-start | bytes 3145736 | tf_op jit(solution)/shard_map/ppermute | solution.py:17
where the time goes:
time: 216 us; the launch traced here: 215 us
  local copies, waits for them, and re-layouts  120 us (56%)
  matrix products  42 us (19%)
  blocking collectives  37.6 us (17%)
  other arithmetic  8.25 us (4%)
  starting transfers between devices  5.27 us (2%)
    reshape x8, local copies, waits for them, and re-layouts, one_block(): banded = tiled.reshape(block, count_rows, span)  75.1 us
    dot_general x8, matrix products, one_block(): jnp.einsum('gcj,gtj->gct', row_part.astype(jnp.float32), banded, precisio...  42 us
    psum x1, blocking collectives, on_device(): gain_grad = lax.psum(jnp.sum(mixed_grad * normed, axis=0), 'ctx')  37.6 us
    while x8, local copies, waits for them, and re-layouts  19.4 us
    slice x8, local copies, waits for them, and re-layouts, one_block(): tiled = jnp.tile(filter_part, (1, count_rows))[:, :count_rows * span]  17.9 us
    unnamed x14, local copies, waits for them, and re-layouts  5.31 us
  transfers between devices with their start and end apart: 2, of which 1 were waited for; matrix products, arithmetic and copies ran while one was open for 1% of the time, Pallas kernels for 0%

commit v1 on v0

v1 whole, which is shorter than its diff:
```python
import functools

import jax
import jax.numpy as jnp
from jax import lax
from jax.experimental import pallas as pl
from jax.experimental.pallas import tpu as pltpu
from jax.sharding import PartitionSpec as P

BLOCKS = 4
LANES = 128
MESH = pl.DeviceIdType.MESH


def kernel(
    n_ctx, n_pipe,
    act_hbm, gate_hbm, up_hbm, filt_ref, gain_ref, ids_ref,
    out_ref, gg_ref,
    act, gate, up, hx, halo, sent, mixed, mask, inv, gacc, gsend, gslots,
    in_sem, hs_sem, hr_sem, ps_sem, pr_sem, gs_sem, gr_sem,
):
    tokens, width = act.shape
    rows = tokens // BLOCKS
    groups, taps = filt_ref.shape
    size = width // groups
    per = LANES // size
    strips = width // LANES
    ctx = lax.axis_index("ctx")
    pipe = lax.axis_index("pipe")
    has_next = ctx < n_ctx - 1
    has_prev = ctx > 0
    behind = lax.rem(pipe + n_pipe - 1, n_pipe)
    ahead = lax.rem(pipe + 1, n_pipe)

    barrier = pltpu.get_barrier_semaphore()
    for d in range(1, n_ctx):
        pl.semaphore_signal(barrier, inc=1, device_id={"ctx": lax.rem(ctx + d, n_ctx)}, device_id_type=MESH)
    pl.semaphore_signal(barrier, inc=1, device_id={"pipe": behind}, device_id_type=MESH)
    pl.semaphore_signal(barrier, inc=1, device_id={"pipe": ahead}, device_id_type=MESH)

    def part(b):
        return pl.ds(b * rows, rows)

    loads = []
    for b in range(BLOCKS):
        loads.append([
            pltpu.make_async_copy(gate_hbm.at[part(b)], gate.at[part(b)], in_sem.at[0, b]),
            pltpu.make_async_copy(up_hbm.at[part(b)], up.at[part(b)], in_sem.at[1, b]),
        ])
    act_load = pltpu.make_async_copy(act_hbm, act, in_sem.at[2, 0])
    for pair in loads:
        for one in pair:
            one.start()
    act_load.start()

    first = pl.multiple_of(ctx * tokens, LANES)
    after = pl.multiple_of(jnp.minimum(ctx + 1, n_ctx - 1) * tokens, LANES)
    own_ids = jnp.broadcast_to(ids_ref[:, pl.ds(first, tokens)].astype(jnp.float32), (tokens, tokens))
    next_ids = jnp.broadcast_to(ids_ref[:, pl.ds(after, tokens)].astype(jnp.float32), (tokens, tokens))
    out_ids = own_ids.T
    row = lax.broadcasted_iota(jnp.int32, (tokens, tokens), 0)
    col = lax.broadcasted_iota(jnp.int32, (tokens, tokens), 1)
    live = jnp.where(has_next, 1.0, 0.0)
    own_mask = jnp.where((col >= row) & (own_ids == out_ids), 1.0, 0.0)
    next_mask = jnp.where((col < row) & (next_ids == out_ids), live, 0.0)
    mask[:, :tokens] = own_mask.astype(jnp.bfloat16)
    mask[:, tokens:] = next_mask.astype(jnp.bfloat16)
    hx[tokens:, :] = jnp.zeros((tokens, width), jnp.bfloat16)
    gacc[...] = jnp.zeros_like(gacc)

    halo_copy = [
        pltpu.make_async_remote_copy(
            src_ref=hx.at[part(b)], dst_ref=halo.at[b], send_sem=hs_sem.at[b], recv_sem=hr_sem.at[b],
            device_id={"ctx": jnp.maximum(ctx - 1, 0)}, device_id_type=MESH)
        for b in range(BLOCKS)
    ]
    pipe_copy = [
        pltpu.make_async_remote_copy(
            src_ref=sent.at[part(b)], dst_ref=out_ref.at[part(b)], send_sem=ps_sem.at[b], recv_sem=pr_sem.at[b],
            device_id={"pipe": behind}, device_id_type=MESH)
        for b in range(BLOCKS)
    ]
    gain_copy = [
        pltpu.make_async_remote_copy(
            src_ref=gsend, dst_ref=gslots.at[ctx], send_sem=gs_sem.at[d], recv_sem=gr_sem.at[d],
            device_id={"ctx": lax.rem(ctx + d, n_ctx)}, device_id_type=MESH)
        for d in range(1, n_ctx)
    ]

    for b in range(BLOCKS):
        for one in loads[b]:
            one.wait()
        hx[part(b), :] = (
            up[part(b), :].astype(jnp.float32) * gate[part(b), :].astype(jnp.float32)
        ).astype(jnp.bfloat16)
        if b == 0:
            pl.semaphore_wait(barrier, n_ctx - 1 + 2)

        @pl.when(has_prev)
        def _():
            halo_copy[b].start()

    act_load.wait()

    def squares(i, total):
        x = act[:, pl.ds(pl.multiple_of(i * LANES, LANES), LANES)].astype(jnp.float32)
        return total + x * x

    total = lax.fori_loop(0, strips, squares, jnp.zeros((tokens, LANES), jnp.float32))
    inv[...] = jnp.broadcast_to(
        lax.rsqrt(jnp.sum(total, axis=1, keepdims=True) * (1.0 / width) + 1e-06), (tokens, LANES))

    lane_group = lax.broadcasted_iota(jnp.int32, (rows, LANES), 1) // size

    for b in range(BLOCKS):
        @pl.when(has_next)
        def _():
            halo_copy[b].wait_recv()
            hx[pl.ds(tokens + b * rows, rows), :] = halo[b]

        def strip(i, dots):
            cols = pl.ds(pl.multiple_of(i * LANES, LANES), LANES)
            taps_here = filt_ref[pl.ds(pl.multiple_of(i * per, per), per), :]
            own_m = mask[part(b), :tokens]
            next_m = mask[part(b), tokens:]
            pieces = []
            for g in range(per):
                ring = pltpu.roll(
                    jnp.broadcast_to(taps_here[g:g + 1, :], (rows, taps)), b * rows, 1, stride=1, stride_axis=0
                ).astype(jnp.bfloat16)
                pieces.append(jnp.concatenate([ring * own_m, ring * next_m], axis=1))
            lhs = jnp.concatenate(pieces, axis=0)
            res = jnp.dot(lhs, hx[:, cols], preferred_element_type=jnp.float32)
            mix = res[:rows]
            for g in range(1, per):
                mix = jnp.where(lane_group == g, res[g * rows:(g + 1) * rows], mix)
            mixed[:, cols] = mix
            normed = act[part(b), cols].astype(jnp.float32) * inv[part(b), :]
            both = mix * normed
            gacc[:, cols] += jnp.sum(both.reshape(rows // 8, 8, LANES), axis=0)
            return dots + both * gain_ref[:, cols]

        dots = lax.fori_loop(0, strips, strip, jnp.zeros((rows, LANES), jnp.float32))
        if b == BLOCKS - 1:
            gsend[...] = jnp.sum(gacc[...], axis=0, keepdims=True)
            gslots[ctx] = gsend[...]
            for one in gain_copy:
                one.start()
        proj = jnp.broadcast_to(jnp.sum(dots, axis=1, keepdims=True) * (1.0 / width), (rows, LANES))

        def finish(i, _):
            cols = pl.ds(pl.multiple_of(i * LANES, LANES), LANES)
            scale = inv[part(b), :]
            normed = act[part(b), cols].astype(jnp.float32) * scale
            inner = mixed[:, cols] * gain_ref[:, cols] - normed * proj
            sent[part(b), cols] = (up[part(b), cols].astype(jnp.float32) + scale * inner).astype(jnp.bfloat16)
            return 0

        lax.fori_loop(0, strips, finish, 0)
        pipe_copy[b].start()

    for one in gain_copy:
        one.wait_recv()
    gg_ref[...] = jnp.sum(gslots[...], axis=0)
    for one in gain_copy:
        one.wait_send()
    for b in range(BLOCKS):
        @pl.when(has_prev)
        def _():
            halo_copy[b].wait_send()
    for one in pipe_copy:
        one.wait()


def solution(mesh):
    n_ctx, n_pipe = mesh.shape["ctx"], mesh.shape["pipe"]

    def on_device(activations, gate_values, out_grad, filters, norm_gain, doc_ids):
        _, tokens, width = activations.shape
        rows = tokens // BLOCKS
        anywhere = pl.BlockSpec(memory_space=pl.ANY)
        vmem = pl.BlockSpec(memory_space=pltpu.VMEM)
        bf16, f32 = jnp.bfloat16, jnp.float32
        grad, gain = pl.pallas_call(
            functools.partial(kernel, n_ctx, n_pipe),
            out_shape=(
                jax.ShapeDtypeStruct((tokens, width), bf16),
                jax.ShapeDtypeStruct((1, width), f32),
            ),
            in_specs=[anywhere] * 3 + [vmem] * 3,
            out_specs=(anywhere, vmem),
            scratch_shapes=[
                pltpu.VMEM((tokens, width), bf16),
                pltpu.VMEM((tokens, width), bf16),
                pltpu.VMEM((tokens, width), bf16),
                pltpu.VMEM((2 * tokens, width), bf16),
                pltpu.VMEM((BLOCKS, rows, width), bf16),
                pltpu.VMEM((tokens, width), bf16),
                pltpu.VMEM((rows, width), f32),
                pltpu.VMEM((tokens, 2 * tokens), bf16),
                pltpu.VMEM((tokens, LANES), f32),
                pltpu.VMEM((8, width), f32),
                pltpu.VMEM((1, width), f32),
                pltpu.VMEM((n_ctx, 1, width), f32),
                pltpu.SemaphoreType.DMA((3, BLOCKS)),
                pltpu.SemaphoreType.DMA((BLOCKS,)),
                pltpu.SemaphoreType.DMA((BLOCKS,)),
                pltpu.SemaphoreType.DMA((BLOCKS,)),
                pltpu.SemaphoreType.DMA((BLOCKS,)),
                pltpu.SemaphoreType.DMA((n_ctx,)),
                pltpu.SemaphoreType.DMA((n_ctx,)),
            ],
            compiler_params=pltpu.CompilerParams(
                collective_id=0, has_side_effects=True, vmem_limit_bytes=48 << 20
            ),
        )(activations[0], gate_values[0], out_grad[0], filters[0], norm_gain, doc_ids)
        return grad[None], gain

    return jax.shard_map(
        on_device,
        mesh=mesh,
        in_specs=(
            P("pipe", "ctx", None),
            P("pipe", "ctx", None),
            P("pipe", "ctx", None),
            P("pipe", None, None),
            P("pipe", None),
            P("pipe", None),
        ),
        out_specs=(P("pipe", "ctx", None), P("pipe", None)),
        check_vma=False,
    )
```

time: 216 us -> 55.7 us (0.26)
  the two profiles are of different devices: /device:TPU:0 before, /device:TPU:1 now
where the time goes in v1:
time: 55.7 us; the launch traced here: 55.3 us
  Pallas kernels  47.1 us (85%)
  local copies, waits for them, and re-layouts  7.55 us (14%)
  between operations  0.65 us (1%)
    pallas_call x1, Pallas kernels, on_device(): pl.pallas_call(functools.partial(kernel, n_ctx, n_pipe), out_shape=(jax.S...  47.1 us
    unnamed x14, local copies, waits for them, and re-layouts  7.55 us

profile of v1, /device:TPU:1, one launch (start us, length us, event | category | flops | bytes accessed | tf_op | source)
XLA Modules:
  0.0 55.3 jit_solution(7801072834062888526)
XLA Ops:
  0.6 0.0 copy-start.5
  0.6 0.7 %copy-done.5 = s32[1,1024]{1,0:T(1,128)S(1)} copy-done((s32[1,1024]{1,0:T(1,128)S(1)}, s32[1,1024]{1,0:T(1,128)}, u32[]{:S(2)}) %copy-start.5) | copy-done | bytes 4120
  1.3 0.0 copy-start
  1.3 1.2 %copy-done = bf16[1,128,4096]{2,1,0:T(8,128)(2,1)S(1)} copy-done((bf16[1,128,4096]{2,1,0:T(8,128)(2,1)S(1)}, bf16[1,128,4096]{2,1,0:T(8,128)(2,1)}, u32[]{:S(2)}) %copy-start) | copy-done | bytes 1048600
  2.5 0.0 copy-start.1
  2.5 1.2 %copy-done.1 = bf16[1,128,4096]{2,1,0:T(8,128)(2,1)S(1)} copy-done((bf16[1,128,4096]{2,1,0:T(8,128)(2,1)S(1)}, bf16[1,128,4096]{2,1,0:T(8,128)(2,1)}, u32[]{:S(2)}) %copy-start.1) | copy-done | bytes 1048600
  3.8 0.0 copy-start.2
  3.8 1.2 %copy-done.2 = bf16[1,128,4096]{2,1,0:T(8,128)(2,1)S(1)} copy-done((bf16[1,128,4096]{2,1,0:T(8,128)(2,1)S(1)}, bf16[1,128,4096]{2,1,0:T(8,128)(2,1)}, u32[]{:S(2)}) %copy-start.2) | copy-done | bytes 1048600
  5.0 0.0 copy-start.3
  5.0 0.9 %copy-done.3 = f32[1,256,128]{2,1,0:T(8,128)S(1)} copy-done((f32[1,256,128]{2,1,0:T(8,128)S(1)}, f32[1,256,128]{2,1,0:T(8,128)}, u32[]{:S(2)}) %copy-start.3) | copy-done | bytes 131096
  5.9 0.0 copy-start.4
  5.9 0.7 %copy-done.4 = f32[1,4096]{1,0:T(1,128)S(1)} copy-done((f32[1,4096]{1,0:T(1,128)S(1)}, f32[1,4096]{1,0:T(1,128)}, u32[]{:S(2)}) %copy-start.4) | copy-done | bytes 16408
  6.6 47.1 %shard_map.77 = (bf16[128,4096]{1,0:T(8,128)(2,1)S(1)}, f32[1,4096]{1,0:T(1,128)S(1)}) custom-call(bf16[128,4096]{1,0:T(8,128)(2,1)S(1)} %bitcast.5, bf16[128,4096]{1,0:T(8,128)(2,1)S(1)} %bitcast.6, bf16[128,4096]{1,0:T(8,128)(2,1)S(1)} %bitcast.7, f32[256,128]{1,0:T(8,128)S(1)} %bitcast.9, f32[1,4096]{1,0:T(1,128)S(1)} %copy-done.4, s32[1,1024]{1,0:T(1,128)S(1)} %copy-done.5), custom_call_target="tpu_custom_call" | custom-call | tf_op jit(solution)/shard_map/pallas_call | solution.py:184
  53.8 1.0 %copy.10 = bf16[1,128,4096]{2,1,0:T(8,128)(2,1)} copy(bf16[1,128,4096]{2,1,0:T(8,128)(2,1)S(1)} %bitcast.8) | data formatting | bytes 2097152
  54.7 0.6 %copy.11 = f32[1,4096]{1,0:T(1,128)} copy(f32[1,4096]{1,0:T(1,128)S(1)} %get-tuple-element.9) | data formatting | bytes 32768
Async XLA Ops:
  0.6 0.7 %copy-start.5 = (s32[1,1024]{1,0:T(1,128)S(1)}, s32[1,1024]{1,0:T(1,128)}, u32[]{:S(2)}) copy-start(s32[1,1024]{1,0:T(1,128)} %ids_ref.1) | copy-start | bytes 12292
  1.3 1.2 %copy-start = (bf16[1,128,4096]{2,1,0:T(8,128)(2,1)S(1)}, bf16[1,128,4096]{2,1,0:T(8,128)(2,1)}, u32[]{:S(2)}) copy-start(bf16[1,128,4096]{2,1,0:T(8,128)(2,1)} %param.6) | copy-start | bytes 3145732
  2.5 1.2 %copy-start.1 = (bf16[1,128,4096]{2,1,0:T(8,128)(2,1)S(1)}, bf16[1,128,4096]{2,1,0:T(8,128)(2,1)}, u32[]{:S(2)}) copy-start(bf16[1,128,4096]{2,1,0:T(8,128)(2,1)} %param.7) | copy-start | bytes 3145732
  3.8 1.2 %copy-start.2 = (bf16[1,128,4096]{2,1,0:T(8,128)(2,1)S(1)}, bf16[1,128,4096]{2,1,0:T(8,128)(2,1)}, u32[]{:S(2)}) copy-start(bf16[1,128,4096]{2,1,0:T(8,128)(2,1)} %param.8) | copy-start | bytes 3145732
  5.0 0.9 %copy-start.3 = (f32[1,256,128]{2,1,0:T(8,128)S(1)}, f32[1,256,128]{2,1,0:T(8,128)}, u32[]{:S(2)}) copy-start(f32[1,256,128]{2,1,0:T(8,128)} %param.9) | copy-start | bytes 393220
  5.9 0.7 %copy-start.4 = (f32[1,4096]{1,0:T(1,128)S(1)}, f32[1,4096]{1,0:T(1,128)}, u32[]{:S(2)}) copy-start(f32[1,4096]{1,0:T(1,128)} %gain_ref.1) | copy-start | bytes 49156

commit v2 on v1

--- a/solution.py
+++ b/solution.py
@@ -14,9 +14,9 @@
 
 def kernel(
     n_ctx, n_pipe,
-    act_hbm, gate_hbm, up_hbm, filt_ref, gain_ref, ids_ref,
+    act_hbm, gate_hbm, up_hbm, filt_hbm, gain_hbm, ids_hbm,
     out_ref, gg_ref,
-    act, gate, up, hx, halo, sent, mixed, mask, inv, gacc, gsend, gslots,
+    act, gate, up, filt_ref, gain_ref, ids_ref, hx, halo, sent, mixed, mask, inv, gacc, gsend, gslots,
     in_sem, hs_sem, hr_sem, ps_sem, pr_sem, gs_sem, gr_sem,
 ):
     tokens, width = act.shape
@@ -47,11 +47,19 @@
             pltpu.make_async_copy(gate_hbm.at[part(b)], gate.at[part(b)], in_sem.at[0, b]),
             pltpu.make_async_copy(up_hbm.at[part(b)], up.at[part(b)], in_sem.at[1, b]),
         ])
-    act_load = pltpu.make_async_copy(act_hbm, act, in_sem.at[2, 0])
+    ids_load = pltpu.make_async_copy(ids_hbm, ids_ref, in_sem.at[2, 1])
+    late_loads = [
+        pltpu.make_async_copy(act_hbm, act, in_sem.at[2, 0]),
+        pltpu.make_async_copy(filt_hbm, filt_ref, in_sem.at[2, 2]),
+        pltpu.make_async_copy(gain_hbm, gain_ref, in_sem.at[2, 3]),
+    ]
+    ids_load.start()
     for pair in loads:
         for one in pair:
             one.start()
-    act_load.start()
+    for one in late_loads:
+        one.start()
+    ids_load.wait()
 
     first = pl.multiple_of(ctx * tokens, LANES)
     after = pl.multiple_of(jnp.minimum(ctx + 1, n_ctx - 1) * tokens, LANES)
@@ -100,7 +108,8 @@
         def _():
             halo_copy[b].start()
 
-    act_load.wait()
+    for one in late_loads:
+        one.wait()
 
     def squares(i, total):
         x = act[:, pl.ds(pl.multiple_of(i * LANES, LANES), LANES)].astype(jnp.float32)
@@ -140,7 +149,7 @@
             gacc[:, cols] += jnp.sum(both.reshape(rows // 8, 8, LANES), axis=0)
             return dots + both * gain_ref[:, cols]
 
-        dots = lax.fori_loop(0, strips, strip, jnp.zeros((rows, LANES), jnp.float32))
+        dots = lax.fori_loop(0, strips, strip, jnp.zeros((rows, LANES), jnp.float32), unroll=8)
         if b == BLOCKS - 1:
             gsend[...] = jnp.sum(gacc[...], axis=0, keepdims=True)
             gslots[ctx] = gsend[...]
@@ -156,7 +165,7 @@
             sent[part(b), cols] = (up[part(b), cols].astype(jnp.float32) + scale * inner).astype(jnp.bfloat16)
             return 0
 
-        lax.fori_loop(0, strips, finish, 0)
+        lax.fori_loop(0, strips, finish, 0, unroll=4)
         pipe_copy[b].start()
 
     for one in gain_copy:
@@ -178,7 +187,9 @@
     def on_device(activations, gate_values, out_grad, filters, norm_gain, doc_ids):
         _, tokens, width = activations.shape
         rows = tokens // BLOCKS
+        groups, taps = filters.shape[1:]
         anywhere = pl.BlockSpec(memory_space=pl.ANY)
+        hbm = pl.BlockSpec(memory_space=pltpu.HBM)
         vmem = pl.BlockSpec(memory_space=pltpu.VMEM)
         bf16, f32 = jnp.bfloat16, jnp.float32
         grad, gain = pl.pallas_call(
@@ -187,12 +198,15 @@
                 jax.ShapeDtypeStruct((tokens, width), bf16),
                 jax.ShapeDtypeStruct((1, width), f32),
             ),
-            in_specs=[anywhere] * 3 + [vmem] * 3,
+            in_specs=[hbm] * 6,
             out_specs=(anywhere, vmem),
             scratch_shapes=[
                 pltpu.VMEM((tokens, width), bf16),
                 pltpu.VMEM((tokens, width), bf16),
                 pltpu.VMEM((tokens, width), bf16),
+                pltpu.VMEM((groups, taps), f32),
+                pltpu.VMEM(norm_gain.shape, f32),
+                pltpu.VMEM(doc_ids.shape, jnp.int32),
                 pltpu.VMEM((2 * tokens, width), bf16),
                 pltpu.VMEM((BLOCKS, rows, width), bf16),
                 pltpu.VMEM((tokens, width), bf16),
@@ -211,7 +225,7 @@
                 pltpu.SemaphoreType.DMA((n_ctx,)),
             ],
             compiler_params=pltpu.CompilerParams(
-                collective_id=0, has_side_effects=True, vmem_limit_bytes=48 << 20
+                collective_id=0, has_side_effects=True, vmem_limit_bytes=67043328
             ),
         )(activations[0], gate_values[0], out_grad[0], filters[0], norm_gain, doc_ids)
         return grad[None], gain

time: 55.7 us -> 38.4 us (0.69)
  Pallas kernels: 47.1 us -> 34.6 us
  local copies, waits for them, and re-layouts: 7.55 us -> 2.9 us
    pallas_call x1, Pallas kernels: 47.1 us -> 34.6 us  [on_device(): pl.pallas_call(functools.partial(kernel, n_ctx, n_pipe), out_shape=(jax.S...]
    unnamed x14 -> x4, local copies, waits for them, and re-layouts: 7.55 us -> 2.9 us
where the time goes in v2:
time: 38.4 us; the launch traced here: 38.2 us
  Pallas kernels  34.6 us (90%)
  local copies, waits for them, and re-layouts  2.9 us (8%)
  between operations  0.65 us (2%)
    pallas_call x1, Pallas kernels, on_device(): pl.pallas_call(functools.partial(kernel, n_ctx, n_pipe), out_shape=(jax.S...  34.6 us
    unnamed x4, local copies, waits for them, and re-layouts  2.9 us

profile of v2, /device:TPU:1, one launch (start us, length us, event | category | flops | bytes accessed | tf_op | source)
XLA Modules:
  0.0 38.2 jit_solution(12124080601932523559)
XLA Ops:
  0.6 34.6 %shard_map.77 = (bf16[128,4096]{1,0:T(8,128)(2,1)}, f32[1,4096]{1,0:T(1,128)}) custom-call(bf16[128,4096]{1,0:T(8,128)(2,1)} %bitcast.5, bf16[128,4096]{1,0:T(8,128)(2,1)} %bitcast.6, bf16[128,4096]{1,0:T(8,128)(2,1)} %bitcast.7, f32[256,128]{1,0:T(8,128)} %bitcast.9, f32[1,4096]{1,0:T(1,128)} %gain_hbm.1, s32[1,1024]{1,0:T(1,128)} %ids_hbm.1), custom_call_target="tpu_custom_call" | custom-call | tf_op jit(solution)/shard_map/pallas_call | solution.py:195
  35.3 0.0 copy-start
  35.3 2.3 %copy.10 = bf16[1,128,4096]{2,1,0:T(8,128)(2,1)} copy(bf16[1,128,4096]{2,1,0:T(8,128)(2,1)} %bitcast.8) | data formatting | bytes 2097152
  37.6 0.0 copy-done
  37.6 0.6 %copy.11 = f32[1,4096]{1,0:T(1,128)} copy(f32[1,4096]{1,0:T(1,128)S(1)} %copy-done) | data formatting | bytes 32768
Async XLA Ops:
  35.3 2.3 %copy-start = (f32[1,4096]{1,0:T(1,128)S(1)}, f32[1,4096]{1,0:T(1,128)}, u32[]{:S(2)}) copy-start(f32[1,4096]{1,0:T(1,128)} %get-tuple-element.9) | copy-start | bytes 49156

commit v3 on v2

v3 whole, which is shorter than its diff:
```python
import functools

import jax
import jax.numpy as jnp
from jax import lax
from jax.experimental import pallas as pl
from jax.experimental.pallas import tpu as pltpu
from jax.sharding import PartitionSpec as P

LANES = 128
MESH = pl.DeviceIdType.MESH


def cuts(tokens):
    step = tokens // 4
    edges = [0, step // 2] + list(range(step, tokens + 1, step))
    return [(a, b - a) for a, b in zip(edges[:-1], edges[1:])]


def kernel(
    n_ctx, n_pipe,
    act_hbm, gate_hbm, up_hbm, filt_hbm, gain_hbm, ids_hbm,
    out_ref, gg_ref,
    act, gate, up, filt_ref, gain_ref, ids_ref, hx, halo, sent, mixed, mask, inv, gacc, gsend, gslots,
    in_sem, hs_sem, hr_sem, ps_sem, pr_sem, gs_sem, gr_sem, wave,
):
    tokens, width = act.shape
    blocks = cuts(tokens)
    count = len(blocks)
    groups, taps = filt_ref.shape
    size = width // groups
    per = LANES // size
    strips = width // LANES
    ctx = lax.axis_index("ctx")
    pipe = lax.axis_index("pipe")
    has_next = ctx < n_ctx - 1
    has_prev = ctx > 0
    behind = lax.rem(pipe + n_pipe - 1, n_pipe)
    ahead = lax.rem(pipe + 1, n_pipe)

    barrier = pltpu.get_barrier_semaphore()
    @pl.when(has_prev)
    def _():
        pl.semaphore_signal(barrier, inc=1, device_id={"ctx": ctx - 1}, device_id_type=MESH)

    @pl.when(has_next)
    def _():
        pl.semaphore_signal(barrier, inc=1, device_id={"ctx": ctx + 1}, device_id_type=MESH)

    pl.semaphore_signal(barrier, inc=1, device_id={"pipe": behind}, device_id_type=MESH)
    pl.semaphore_signal(barrier, inc=1, device_id={"pipe": ahead}, device_id_type=MESH)

    def part(b):
        return pl.ds(*blocks[b])

    loads = []
    for b in range(count):
        loads.append([
            pltpu.make_async_copy(gate_hbm.at[part(b)], gate.at[part(b)], in_sem.at[0, b]),
            pltpu.make_async_copy(up_hbm.at[part(b)], up.at[part(b)], in_sem.at[1, b]),
        ])
    ids_load = pltpu.make_async_copy(ids_hbm, ids_ref, in_sem.at[2, 1])
    late_loads = [
        pltpu.make_async_copy(act_hbm, act, in_sem.at[2, 0]),
        pltpu.make_async_copy(filt_hbm, filt_ref, in_sem.at[2, 2]),
        pltpu.make_async_copy(gain_hbm, gain_ref, in_sem.at[2, 3]),
    ]
    for pair in loads:
        for one in pair:
            one.start()
    ids_load.start()
    for one in late_loads:
        one.start()
    halo_copy = [
        pltpu.make_async_remote_copy(
            src_ref=hx.at[part(b)], dst_ref=halo.at[part(b)], send_sem=hs_sem.at[b], recv_sem=hr_sem.at[b],
            device_id={"ctx": jnp.maximum(ctx - 1, 0)}, device_id_type=MESH)
        for b in range(count)
    ]
    pipe_copy = [
        pltpu.make_async_remote_copy(
            src_ref=sent.at[part(b)], dst_ref=out_ref.at[part(b)], send_sem=ps_sem.at[b], recv_sem=pr_sem.at[b],
            device_id={"pipe": behind}, device_id_type=MESH)
        for b in range(count)
    ]
    gain_copy = [
        pltpu.make_async_remote_copy(
            src_ref=gsend, dst_ref=gslots.at[ctx], send_sem=gs_sem.at[d], recv_sem=gr_sem.at[d],
            device_id={"ctx": lax.rem(ctx + d, n_ctx)}, device_id_type=MESH)
        for d in range(1, n_ctx)
    ]

    for b in range(count):
        for one in loads[b]:
            one.wait()
        hx[part(b), :] = (
            up[part(b), :].astype(jnp.float32) * gate[part(b), :].astype(jnp.float32)
        ).astype(jnp.bfloat16)
        if b == 0:
            pl.semaphore_wait(barrier, 2 + has_prev.astype(jnp.int32) + has_next.astype(jnp.int32))

        @pl.when(has_prev)
        def _():
            halo_copy[b].start()

    ids_load.wait()

    first = pl.multiple_of(ctx * tokens, LANES)
    after = pl.multiple_of(jnp.minimum(ctx + 1, n_ctx - 1) * tokens, LANES)
    own_ids = jnp.broadcast_to(ids_ref[:, pl.ds(first, tokens)].astype(jnp.float32), (tokens, tokens))
    next_ids = jnp.broadcast_to(ids_ref[:, pl.ds(after, tokens)].astype(jnp.float32), (tokens, tokens))
    out_ids = own_ids.T
    row = lax.broadcasted_iota(jnp.int32, (tokens, tokens), 0)
    col = lax.broadcasted_iota(jnp.int32, (tokens, tokens), 1)
    live = jnp.where(has_next, 1.0, 0.0)
    own_mask = jnp.where((col >= row) & (own_ids == out_ids), 1.0, 0.0)
    next_mask = jnp.where((col < row) & (next_ids == out_ids), live, 0.0)
    mask[:, :tokens] = own_mask.astype(jnp.bfloat16)
    mask[:, tokens:] = next_mask.astype(jnp.bfloat16)
    hx[tokens:, :] = jnp.zeros((tokens, width), jnp.bfloat16)
    gacc[...] = jnp.zeros_like(gacc)

    for one in late_loads:
        one.wait()

    def squares(i, total):
        x = act[:, pl.ds(pl.multiple_of(i * LANES, LANES), LANES)].astype(jnp.float32)
        return total + x * x

    total = lax.fori_loop(0, strips, squares, jnp.zeros((tokens, LANES), jnp.float32))
    inv[...] = jnp.broadcast_to(
        lax.rsqrt(jnp.sum(total, axis=1, keepdims=True) * (1.0 / width) + 1e-06), (tokens, LANES))

    for b in range(count):
        start, rows = blocks[b]
        lane_group = lax.broadcasted_iota(jnp.int32, (rows, LANES), 1) // size

        @pl.when(has_next)
        def _():
            halo_copy[b].wait_recv()
            hx[pl.ds(tokens + start, rows), :] = halo[part(b), :]

        def strip(i, dots):
            cols = pl.ds(pl.multiple_of(i * LANES, LANES), LANES)
            taps_here = filt_ref[pl.ds(pl.multiple_of(i * per, per), per), :]
            own_m = mask[part(b), :tokens]
            next_m = mask[part(b), tokens:]
            pieces = []
            for g in range(per):
                ring = pltpu.roll(
                    jnp.broadcast_to(taps_here[g:g + 1, :], (rows, taps)), start, 1, stride=1, stride_axis=0
                ).astype(jnp.bfloat16)
                pieces.append(jnp.concatenate([ring * own_m, ring * next_m], axis=1))
            lhs = jnp.concatenate(pieces, axis=0)
            res = jnp.dot(lhs, hx[:, cols], preferred_element_type=jnp.float32)
            mix = res[:rows]
            for g in range(1, per):
                mix = jnp.where(lane_group == g, res[g * rows:(g + 1) * rows], mix)
            mixed[:rows, cols] = mix
            normed = act[part(b), cols].astype(jnp.float32) * inv[part(b), :]
            both = mix * normed
            gacc[:, cols] += jnp.sum(both.reshape(rows // 8, 8, LANES), axis=0)
            return dots + both * gain_ref[:, cols]

        dots = lax.fori_loop(0, strips, strip, jnp.zeros((rows, LANES), jnp.float32), unroll=8)
        if b == count - 1:
            gsend[...] = jnp.sum(gacc[...], axis=0, keepdims=True)
            gslots[ctx] = gsend[...]
        proj = jnp.broadcast_to(jnp.sum(dots, axis=1, keepdims=True) * (1.0 / width), (rows, LANES))

        def finish(i, _):
            cols = pl.ds(pl.multiple_of(i * LANES, LANES), LANES)
            scale = inv[part(b), :]
            normed = act[part(b), cols].astype(jnp.float32) * scale
            inner = mixed[:rows, cols] * gain_ref[:, cols] - normed * proj
            sent[part(b), cols] = (up[part(b), cols].astype(jnp.float32) + scale * inner).astype(jnp.bfloat16)
            return 0

        lax.fori_loop(0, strips, finish, 0, unroll=4)
        pipe_copy[b].start()

    @pl.when(has_next)
    def _():
        pl.semaphore_wait(wave.at[0], 1)

    @pl.when(has_prev)
    def _():
        pl.semaphore_signal(wave.at[0], inc=1, device_id={"ctx": ctx - 1}, device_id_type=MESH)
        pl.semaphore_wait(wave.at[1], 1)

    @pl.when(has_next)
    def _():
        pl.semaphore_signal(wave.at[1], inc=1, device_id={"ctx": ctx + 1}, device_id_type=MESH)

    for one in gain_copy:
        one.start()
    for one in gain_copy:
        one.wait_recv()
    gg_ref[...] = jnp.sum(gslots[...], axis=0)
    for one in gain_copy:
        one.wait_send()
    for b in range(count):
        @pl.when(has_prev)
        def _():
            halo_copy[b].wait_send()
    for one in pipe_copy:
        one.wait()


def solution(mesh):
    n_ctx, n_pipe = mesh.shape["ctx"], mesh.shape["pipe"]

    def on_device(activations, gate_values, out_grad, filters, norm_gain, doc_ids):
        _, tokens, width = activations.shape
        count = len(cuts(tokens))
        most = max(rows for _, rows in cuts(tokens))
        groups, taps = filters.shape[1:]
        anywhere = pl.BlockSpec(memory_space=pl.ANY)
        hbm = pl.BlockSpec(memory_space=pltpu.HBM)
        vmem = pl.BlockSpec(memory_space=pltpu.VMEM)
        bf16, f32 = jnp.bfloat16, jnp.float32
        grad, gain = pl.pallas_call(
            functools.partial(kernel, n_ctx, n_pipe),
            out_shape=(
                pltpu.VMEM((tokens, width), bf16),
                pltpu.VMEM((1, width), f32),
            ),
            in_specs=[hbm] * 6,
            out_specs=(vmem, vmem),
            scratch_shapes=[
                pltpu.VMEM((tokens, width), bf16),
                pltpu.VMEM((tokens, width), bf16),
                pltpu.VMEM((tokens, width), bf16),
                pltpu.VMEM((groups, taps), f32),
                pltpu.VMEM(norm_gain.shape, f32),
                pltpu.VMEM(doc_ids.shape, jnp.int32),
                pltpu.VMEM((2 * tokens, width), bf16),
                pltpu.VMEM((tokens, width), bf16),
                pltpu.VMEM((tokens, width), bf16),
                pltpu.VMEM((most, width), f32),
                pltpu.VMEM((tokens, 2 * tokens), bf16),
                pltpu.VMEM((tokens, LANES), f32),
                pltpu.VMEM((8, width), f32),
                pltpu.VMEM((1, width), f32),
                pltpu.VMEM((n_ctx, 1, width), f32),
                pltpu.SemaphoreType.DMA((3, count)),
                pltpu.SemaphoreType.DMA((count,)),
                pltpu.SemaphoreType.DMA((count,)),
                pltpu.SemaphoreType.DMA((count,)),
                pltpu.SemaphoreType.DMA((count,)),
                pltpu.SemaphoreType.DMA((n_ctx,)),
                pltpu.SemaphoreType.DMA((n_ctx,)),
                pltpu.SemaphoreType.REGULAR((2,)),
            ],
            compiler_params=pltpu.CompilerParams(
                collective_id=0, has_side_effects=True, vmem_limit_bytes=60 << 20
            ),
        )(*[
            pltpu.with_memory_space_constraint(x, pltpu.HBM)
            for x in (activations[0], gate_values[0], out_grad[0], filters[0], norm_gain, doc_ids)
        ])
        return grad[None], gain

    return jax.shard_map(
        on_device,
        mesh=mesh,
        in_specs=(
            P("pipe", "ctx", None),
            P("pipe", "ctx", None),
            P("pipe", "ctx", None),
            P("pipe", None, None),
            P("pipe", None),
            P("pipe", None),
        ),
        out_specs=(P("pipe", "ctx", None), P("pipe", None)),
        check_vma=False,
    )
```

time: 38.4 us -> 34.4 us (0.90)
  Pallas kernels: 34.6 us -> 31.7 us
  local copies, waits for them, and re-layouts: 2.9 us -> 1.58 us
    pallas_call x1, Pallas kernels: 34.6 us -> 31.7 us  [on_device(): pl.pallas_call(functools.partial(kernel, n_ctx, n_pipe), out_shape=(pltpu...]
    unnamed x4 -> x2, local copies, waits for them, and re-layouts: 2.9 us -> 1.58 us
where the time goes in v3:
time: 34.4 us; the launch traced here: 33.9 us
  Pallas kernels  31.7 us (92%)
  local copies, waits for them, and re-layouts  1.58 us (5%)
  between operations  0.64 us (2%)
    pallas_call x1, Pallas kernels, on_device(): pl.pallas_call(functools.partial(kernel, n_ctx, n_pipe), out_shape=(pltpu...  31.7 us
    unnamed x2, local copies, waits for them, and re-layouts  1.58 us

profile of v3, /device:TPU:1, one launch (start us, length us, event | category | flops | bytes accessed | tf_op | source)
XLA Modules:
  0.0 33.9 jit_solution(711597261627179698)
XLA Ops:
  0.6 31.7 %shard_map.77 = (bf16[128,4096]{1,0:T(8,128)(2,1)S(1)}, f32[1,4096]{1,0:T(1,128)S(1)}) custom-call(bf16[128,4096]{1,0:T(8,128)(2,1)} %bitcast.6, bf16[128,4096]{1,0:T(8,128)(2,1)} %bitcast.7, bf16[128,4096]{1,0:T(8,128)(2,1)} %bitcast.8, f32[256,128]{1,0:T(8,128)} %bitcast.9, f32[1,4096]{1,0:T(1,128)} %gain_hbm.1, s32[1,1024]{1,0:T(1,128)} %ids_hbm.1), custom_call_target="tpu_custom_call" | custom-call | tf_op jit(solution)/shard_map/pallas_call | solution.py:222
  32.3 1.0 %copy.10 = bf16[1,128,4096]{2,1,0:T(8,128)(2,1)} copy(bf16[1,128,4096]{2,1,0:T(8,128)(2,1)S(1)} %bitcast.5) | data formatting | bytes 2097152
  33.3 0.6 %copy.11 = f32[1,4096]{1,0:T(1,128)} copy(f32[1,4096]{1,0:T(1,128)S(1)} %get-tuple-element.7) | data formatting | bytes 32768

commit v4 on v3

--- a/solution.py
+++ b/solution.py
@@ -127,7 +127,7 @@
         x = act[:, pl.ds(pl.multiple_of(i * LANES, LANES), LANES)].astype(jnp.float32)
         return total + x * x
 
-    total = lax.fori_loop(0, strips, squares, jnp.zeros((tokens, LANES), jnp.float32))
+    total = lax.fori_loop(0, strips, squares, jnp.zeros((tokens, LANES), jnp.float32), unroll=8)
     inv[...] = jnp.broadcast_to(
         lax.rsqrt(jnp.sum(total, axis=1, keepdims=True) * (1.0 / width) + 1e-06), (tokens, LANES))
 
@@ -204,6 +204,18 @@
         def _():
             halo_copy[b].wait_send()
     for one in pipe_copy:
+        one.wait()
+
+
+def deliver(grad_ref, gain_ref, out_hbm, gg_hbm, sem):
+    quarter = grad_ref.shape[0] // 4
+    copies = [pltpu.make_async_copy(gain_ref, gg_hbm, sem.at[4])]
+    for q in range(4):
+        at = pl.ds(q * quarter, quarter)
+        copies.append(pltpu.make_async_copy(grad_ref.at[at], out_hbm.at[at], sem.at[q]))
+    for one in copies:
+        one.start()
+    for one in copies:
         one.wait()
 
 
@@ -259,6 +271,17 @@
             pltpu.with_memory_space_constraint(x, pltpu.HBM)
             for x in (activations[0], gate_values[0], out_grad[0], filters[0], norm_gain, doc_ids)
         ])
+        grad, gain = pl.pallas_call(
+            deliver,
+            out_shape=(
+                jax.ShapeDtypeStruct((tokens, width), bf16),
+                jax.ShapeDtypeStruct((1, width), f32),
+            ),
+            in_specs=[vmem] * 2,
+            out_specs=[hbm] * 2,
+            scratch_shapes=[pltpu.SemaphoreType.DMA((5,))],
+            compiler_params=pltpu.CompilerParams(vmem_limit_bytes=1 << 20),
+        )(*[pltpu.with_memory_space_constraint(x, pltpu.VMEM) for x in (grad, gain)])
         return grad[None], gain
 
     return jax.shard_map(

time: 34.4 us -> 33.8 us (0.983)
  local copies, waits for them, and re-layouts: 1.58 us -> 0 us
  Pallas kernels: 31.7 us -> 32.7 us
    unnamed x2 -> x0, local copies, waits for them, and re-layouts: 1.58 us -> none
    pallas_call x0 -> x1, Pallas kernels: none -> 1.01 us  [on_device(): pl.pallas_call(deliver, out_shape=(jax.ShapeDtypeStruct((tokens, width),...]
where the time goes in v4:
time: 33.8 us; the launch traced here: 33.4 us
  Pallas kernels  32.7 us (97%)
  between operations  0.64 us (2%)
    pallas_call x1, Pallas kernels, on_device(): pl.pallas_call(functools.partial(kernel, n_ctx, n_pipe), out_shape=(pltpu...  31.7 us
    pallas_call x1, Pallas kernels, on_device(): pl.pallas_call(deliver, out_shape=(jax.ShapeDtypeStruct((tokens, width),...  1.01 us

profile of v4, /device:TPU:1, one launch (start us, length us, event | category | flops | bytes accessed | tf_op | source)
XLA Modules:
  0.0 33.4 jit_solution(12052315674098514353)
XLA Ops:
  0.6 31.7 %shard_map.77 = (bf16[128,4096]{1,0:T(8,128)(2,1)S(1)}, f32[1,4096]{1,0:T(1,128)S(1)}) custom-call(bf16[128,4096]{1,0:T(8,128)(2,1)} %bitcast.5, bf16[128,4096]{1,0:T(8,128)(2,1)} %bitcast.6, bf16[128,4096]{1,0:T(8,128)(2,1)} %bitcast.7, f32[256,128]{1,0:T(8,128)} %bitcast.8, f32[1,4096]{1,0:T(1,128)} %gain_hbm.1, s32[1,1024]{1,0:T(1,128)} %ids_hbm.1), custom_call_target="tpu_custom_call" | custom-call | tf_op jit(solution)/shard_map/pallas_call | solution.py:234
  32.3 1.0 %shard_map.78 = (bf16[128,4096]{1,0:T(8,128)(2,1)}, f32[1,4096]{1,0:T(1,128)}) custom-call(bf16[128,4096]{1,0:T(8,128)(2,1)S(1)} %get-tuple-element.6.grad_ref, f32[1,4096]{1,0:T(1,128)S(1)} %get-tuple-element.7.gain_ref), custom_call_target="tpu_custom_call" | custom-call | tf_op jit(solution)/shard_map/pallas_call | solution.py:274

commit v5 on v4

--- a/solution.py
+++ b/solution.py
@@ -71,6 +71,9 @@
     ids_load.start()
     for one in late_loads:
         one.start()
+    hx[tokens:, :] = jnp.zeros((tokens, width), jnp.bfloat16)
+    gacc[...] = jnp.zeros_like(gacc)
+
     halo_copy = [
         pltpu.make_async_remote_copy(
             src_ref=hx.at[part(b)], dst_ref=halo.at[part(b)], send_sem=hs_sem.at[b], recv_sem=hr_sem.at[b],
@@ -117,8 +120,6 @@
     next_mask = jnp.where((col < row) & (next_ids == out_ids), live, 0.0)
     mask[:, :tokens] = own_mask.astype(jnp.bfloat16)
     mask[:, tokens:] = next_mask.astype(jnp.bfloat16)
-    hx[tokens:, :] = jnp.zeros((tokens, width), jnp.bfloat16)
-    gacc[...] = jnp.zeros_like(gacc)
 
     for one in late_loads:
         one.wait()
@@ -162,7 +163,7 @@
             gacc[:, cols] += jnp.sum(both.reshape(rows // 8, 8, LANES), axis=0)
             return dots + both * gain_ref[:, cols]
 
-        dots = lax.fori_loop(0, strips, strip, jnp.zeros((rows, LANES), jnp.float32), unroll=8)
+        dots = lax.fori_loop(0, strips, strip, jnp.zeros((rows, LANES), jnp.float32), unroll=16)
         if b == count - 1:
             gsend[...] = jnp.sum(gacc[...], axis=0, keepdims=True)
             gslots[ctx] = gsend[...]

time: 33.8 us -> 33.4 us (0.988)
  Pallas kernels: 32.7 us -> 32.3 us
    pallas_call x1, Pallas kernels: 31.7 us -> 31.2 us  [on_device(): pl.pallas_call(functools.partial(kernel, n_ctx, n_pipe), out_shape=(pltpu...]
where the time goes in v5:
time: 33.4 us; the launch traced here: 32.9 us
  Pallas kernels  32.3 us (97%)
  between operations  0.64 us (2%)
    pallas_call x1, Pallas kernels, on_device(): pl.pallas_call(functools.partial(kernel, n_ctx, n_pipe), out_shape=(pltpu...  31.2 us
    pallas_call x1, Pallas kernels, on_device(): pl.pallas_call(deliver, out_shape=(jax.ShapeDtypeStruct((tokens, width),...  1.01 us

profile of v5, /device:TPU:1, one launch (start us, length us, event | category | flops | bytes accessed | tf_op | source)
XLA Modules:
  0.0 32.9 jit_solution(2891913551339078137)
XLA Ops:
  0.6 31.2 %shard_map.77 = (bf16[128,4096]{1,0:T(8,128)(2,1)S(1)}, f32[1,4096]{1,0:T(1,128)S(1)}) custom-call(bf16[128,4096]{1,0:T(8,128)(2,1)} %bitcast.5, bf16[128,4096]{1,0:T(8,128)(2,1)} %bitcast.6, bf16[128,4096]{1,0:T(8,128)(2,1)} %bitcast.7, f32[256,128]{1,0:T(8,128)} %bitcast.8, f32[1,4096]{1,0:T(1,128)} %gain_hbm.1, s32[1,1024]{1,0:T(1,128)} %ids_hbm.1), custom_call_target="tpu_custom_call" | custom-call | tf_op jit(solution)/shard_map/pallas_call | solution.py:235
  31.9 1.0 %shard_map.78 = (bf16[128,4096]{1,0:T(8,128)(2,1)}, f32[1,4096]{1,0:T(1,128)}) custom-call(bf16[128,4096]{1,0:T(8,128)(2,1)S(1)} %get-tuple-element.6.grad_ref, f32[1,4096]{1,0:T(1,128)S(1)} %get-tuple-element.7.gain_ref), custom_call_target="tpu_custom_call" | custom-call | tf_op jit(solution)/shard_map/pallas_call | solution.py:275

commit v6 on v5

--- a/solution.py
+++ b/solution.py
@@ -124,17 +124,17 @@
     for one in late_loads:
         one.wait()
 
-    def squares(i, total):
-        x = act[:, pl.ds(pl.multiple_of(i * LANES, LANES), LANES)].astype(jnp.float32)
-        return total + x * x
-
-    total = lax.fori_loop(0, strips, squares, jnp.zeros((tokens, LANES), jnp.float32), unroll=8)
-    inv[...] = jnp.broadcast_to(
-        lax.rsqrt(jnp.sum(total, axis=1, keepdims=True) * (1.0 / width) + 1e-06), (tokens, LANES))
-
     for b in range(count):
         start, rows = blocks[b]
         lane_group = lax.broadcasted_iota(jnp.int32, (rows, LANES), 1) // size
+
+        def squares(i, total):
+            x = act[part(b), pl.ds(pl.multiple_of(i * LANES, LANES), LANES)].astype(jnp.float32)
+            return total + x * x
+
+        total = lax.fori_loop(0, strips, squares, jnp.zeros((rows, LANES), jnp.float32), unroll=8)
+        inv[part(b), :] = jnp.broadcast_to(
+            lax.rsqrt(jnp.sum(total, axis=1, keepdims=True) * (1.0 / width) + 1e-06), (rows, LANES))
 
         @pl.when(has_next)
         def _():

time: 33.4 us -> 33.4 us (level)
  no operation moved by 1% of the time
where the time goes in v6:
time: 33.4 us; the launch traced here: 32.9 us
  Pallas kernels  32.3 us (97%)
  between operations  0.64 us (2%)
    pallas_call x1, Pallas kernels, on_device(): pl.pallas_call(functools.partial(kernel, n_ctx, n_pipe), out_shape=(pltpu...  31.2 us
    pallas_call x1, Pallas kernels, on_device(): pl.pallas_call(deliver, out_shape=(jax.ShapeDtypeStruct((tokens, width),...  1.01 us

profile of v6, /device:TPU:1, one launch (start us, length us, event | category | flops | bytes accessed | tf_op | source)
XLA Modules:
  0.0 32.9 jit_solution(5740438991659885035)
XLA Ops:
  0.6 31.2 %shard_map.77 = (bf16[128,4096]{1,0:T(8,128)(2,1)S(1)}, f32[1,4096]{1,0:T(1,128)S(1)}) custom-call(bf16[128,4096]{1,0:T(8,128)(2,1)} %bitcast.5, bf16[128,4096]{1,0:T(8,128)(2,1)} %bitcast.6, bf16[128,4096]{1,0:T(8,128)(2,1)} %bitcast.7, f32[256,128]{1,0:T(8,128)} %bitcast.8, f32[1,4096]{1,0:T(1,128)} %gain_hbm.1, s32[1,1024]{1,0:T(1,128)} %ids_hbm.1), custom_call_target="tpu_custom_call" | custom-call | tf_op jit(solution)/shard_map/pallas_call | solution.py:235
  31.9 1.0 %shard_map.78 = (bf16[128,4096]{1,0:T(8,128)(2,1)}, f32[1,4096]{1,0:T(1,128)}) custom-call(bf16[128,4096]{1,0:T(8,128)(2,1)S(1)} %get-tuple-element.6.grad_ref, f32[1,4096]{1,0:T(1,128)S(1)} %get-tuple-element.7.gain_ref), custom_call_target="tpu_custom_call" | custom-call | tf_op jit(solution)/shard_map/pallas_call | solution.py:275
